TPU v7x, 128 devices: a whole 4x4x4 slice. The times are simulated.
128 devices in a mesh: seq: 8 (over x_lo, z), exp: 16 (over x_hi, y, core).
Axes of the slice: x: 4 (x_hi: 2, x_lo: 2; x = x_hi * 2 + x_lo), y: 4, z: 4, core: 2. Of those that a mesh axis runs over, the one named last changes fastest.
Arguments:
- tokens: bfloat16 [16, 1024, 2048], P('exp', 'seq'), may hold values from -6 to 6
- position_of_row: int32 [16, 1024], P('exp'), may hold values from 0 to 1023, each once within a row
- request_of_position: int32 [16, 1024], P('exp'), may hold values from 0 to 3, never falling along the last dimension, each value on 1 to 512 neighbouring positions
- expert_ids: int32 [16, 1024, 6], P('exp', 'seq'), may hold values from 0 to 63, all different within a row; in each aligned block of 128 rows (0 to 127, 128 to 255, ..., all dimensions but the last counted through in order) at most 16 rows name the same one
- gate_values: float32 [16, 1024, 6], P('exp', 'seq'), may hold values from 0.1 to 1
- attn_norm: bfloat16 [2048], replicated, may hold values from 0.25 to 1.75
- moe_norm: bfloat16 [2048], replicated, may hold values from 0.25 to 1.75
- w_query: bfloat16 [2048, 2048], P(None, 'seq'), may hold values from -0.125 to 0.125
- w_latent: bfloat16 [2048, 512], replicated, may hold values from -0.125 to 0.125
- w_key_up: bfloat16 [512, 2048], P(None, 'seq'), may hold values from -120 to 120
- w_value_up: bfloat16 [512, 2048], P(None, 'seq'), may hold values from -0.25 to 0.25
- w_output: bfloat16 [2048, 2048], P('seq'), may hold values from -0.125 to 0.125
- w_shared_gate: bfloat16 [2048, 2816], P(None, 'seq'), may hold values from -0.125 to 0.125
- w_shared_up: bfloat16 [2048, 2816], P(None, 'seq'), may hold values from -0.125 to 0.125
- w_shared_down: bfloat16 [2816, 2048], P('seq'), may hold values from -0.109375 to 0.109375
- w_routed_gate: bfloat16 [128, 2048, 704], P(('seq', 'exp')), may hold values from -0.125 to 0.125
- w_routed_up: bfloat16 [128, 2048, 704], P(('seq', 'exp')), may hold values from -0.125 to 0.125
- w_routed_down: bfloat16 [128, 704, 2048], P(('seq', 'exp')), may hold values from -0.15625 to 0.15625
Outputs:
- layer_out: bfloat16 [16, 1024, 2048], P('exp', 'seq')
Inputs may be any that keep to these rules, and one draw needn't show every extreme that they name: `expert_ids`: each row names 6 different experts; among the rows of one device no expert is named by more than 16 rows, and some expert reaches 16 on some device. `position_of_row`: each row of a group holds a different position. `request_of_position`: never falls along positions; each request holds 1 to 512 positions.
All inputs are finite; a program needn't handle non-finite values.
Results may differ from a plain program's by a relative error of at most 0.027.
The roundings to bfloat16 on the way count: a program that leaves them out, or rounds other values in their place, can miss the bound.
Values may be sent and summed in bfloat16 or wider, within the bound.
No kernel may reach another device: no remote copies, remote signals or barrier semaphores. Data moves between devices by JAX's collectives and lax.ppermute only.
A program may use at most 128 MiB of HBM per device.

v0:
```python
import jax
import jax.numpy as jnp
from jax import lax
from jax.sharding import PartitionSpec as P

HD = 128
LAT = 512
epsilon = 1e-06
score_scale = 192.0 ** (-0.5)


def rms_scale(values, gain):
    widened = values.astype(jnp.float32)
    mean_square = jnp.mean(widened * widened, axis=-1, keepdims=True)
    return (widened * lax.rsqrt(mean_square + epsilon) * gain.astype(jnp.float32)).astype(
        jnp.bfloat16
    )


def swiglu_rows(rows_in, gate_weight, up_weight):
    gate_proj = jnp.dot(rows_in, gate_weight, preferred_element_type=jnp.float32)
    up_proj = jnp.dot(rows_in, up_weight, preferred_element_type=jnp.float32)
    return (jax.nn.silu(gate_proj) * up_proj).astype(jnp.bfloat16)


def shards(
    tokens,
    position_of_row,
    request_of_position,
    expert_ids,
    gate_values,
    attn_norm,
    moe_norm,
    w_query,
    w_latent,
    w_key_up,
    w_value_up,
    w_output,
    w_shared_gate,
    w_shared_up,
    w_shared_down,
    w_routed_gate,
    w_routed_up,
    w_routed_down,
):
    rows_here = tokens[0]
    row_count = rows_here.shape[0]
    width = rows_here.shape[1]
    heads_here = w_query.shape[1] // HD
    normed = rms_scale(rows_here, attn_norm)
    piece_rows = lax.all_gather(normed, "seq", axis=0, tiled=True)
    queries = jnp.dot(piece_rows, w_query, preferred_element_type=jnp.float32).astype(jnp.bfloat16)
    queries = queries.reshape(piece_rows.shape[0], heads_here, HD)
    key_heads = w_key_up.reshape(LAT, heads_here, HD)
    queries_query_latent = jnp.einsum(
        "rhk,lhk->rhl", queries, key_heads, preferred_element_type=jnp.float32
    ).astype(jnp.bfloat16)
    query_all = queries_query_latent.reshape(piece_rows.shape[0], heads_here * LAT)
    latent_own = jnp.dot(normed, w_latent, preferred_element_type=jnp.float32).astype(jnp.bfloat16)
    latent_all = lax.all_gather(latent_own, "seq", axis=0, tiled=True)
    positions = position_of_row[0]
    requests = jnp.take(request_of_position[0], positions)
    allowed = (requests[:, None] == requests[None, :]) & (positions[None, :] <= positions[:, None])
    head_outputs = []
    for head in range(heads_here):
        query_latent = query_all[:, head * LAT : (head + 1) * LAT]
        scores = (
            jnp.dot(query_latent, latent_all.T, preferred_element_type=jnp.float32) * score_scale
        )
        scores = jnp.where(allowed, scores, -1e30)
        largest = jnp.max(scores, axis=1, keepdims=True)
        raised = jnp.exp(scores - largest)
        probs = (raised / jnp.sum(raised, axis=1, keepdims=True)).astype(jnp.bfloat16)
        mixed = jnp.dot(probs, latent_all, preferred_element_type=jnp.float32).astype(jnp.bfloat16)
        value_head = w_value_up[:, head * HD : (head + 1) * HD]
        head_outputs.append(
            jnp.dot(mixed, value_head, preferred_element_type=jnp.float32).astype(jnp.bfloat16)
        )
    joined = jnp.concatenate(head_outputs, axis=1)
    row_block = joined
    attended = lax.psum_scatter(
        jnp.dot(row_block, w_output, preferred_element_type=jnp.float32),
        "seq",
        scatter_dimension=0,
        tiled=True,
    )
    resid = (rows_here.astype(jnp.float32) + attended).astype(jnp.bfloat16)
    moe_in = rms_scale(resid, moe_norm)
    shared_hidden = swiglu_rows(
        lax.all_gather(moe_in, "seq", axis=0, tiled=True), w_shared_gate, w_shared_up
    )
    row_block = shared_hidden
    shared_out = lax.psum_scatter(
        jnp.dot(row_block, w_shared_down, preferred_element_type=jnp.float32).astype(jnp.bfloat16),
        "seq",
        scatter_dimension=0,
        tiled=True,
    ).astype(jnp.float32)
    seq_count = lax.axis_size("seq")
    exp_count = lax.axis_size("exp")
    devices = seq_count * exp_count
    experts = devices // 2
    highest = expert_ids.shape[2]
    capacity = row_count * highest * 4 // (3 * experts)
    expert_list = expert_ids[0].reshape(row_count * highest)
    onehot = (expert_list[:, None] == jnp.arange(experts, dtype=jnp.int32)[None, :]).astype(
        jnp.int32
    )
    earlier = jnp.cumsum(onehot, axis=0) - onehot
    slot_index = jnp.sum(earlier * onehot, axis=1)
    place = expert_list * capacity + slot_index
    outgoing = (
        jnp.zeros((experts * capacity, width), jnp.bfloat16)
        .at[place]
        .set(jnp.repeat(moe_in, highest, axis=0))
    )
    doubled = jnp.repeat(outgoing.reshape(experts, capacity, width), 2, axis=0)
    arrived = lax.all_to_all(doubled, ("seq", "exp"), split_axis=0, concat_axis=0, tiled=True)
    flattened = arrived.reshape(-1, width)
    activated = swiglu_rows(flattened, w_routed_gate[0], w_routed_up[0])
    half_out = jnp.dot(activated, w_routed_down[0], preferred_element_type=jnp.float32).astype(
        jnp.bfloat16
    )
    partial_value = half_out.reshape(arrived.shape)
    returned = lax.all_to_all(
        partial_value, ("seq", "exp"), split_axis=0, concat_axis=0, tiled=True
    )
    halves = returned.reshape(experts, 2, capacity, width).astype(jnp.float32)
    expert_out = (halves[:, 0] + halves[:, 1]).astype(jnp.bfloat16)
    picked = jnp.take(expert_out.reshape(experts * capacity, width), place, axis=0)
    picked = picked.astype(jnp.float32).reshape(row_count, highest, width)
    routed_out = jnp.sum(picked * gate_values[0][:, :, None], axis=1)
    layer_out = (resid.astype(jnp.float32) + shared_out + routed_out).astype(jnp.bfloat16)
    return layer_out.reshape(1, row_count, width)


def solution(mesh):
    in_specs = (
        P("exp", "seq", None),
        P("exp", None),
        P("exp", None),
        P("exp", "seq", None),
        P("exp", "seq", None),
        P(),
        P(),
        P(None, "seq"),
        P(),
        P(None, "seq"),
        P(None, "seq"),
        P("seq", None),
        P(None, "seq"),
        P(None, "seq"),
        P("seq", None),
        P(("seq", "exp"), None, None),
        P(("seq", "exp"), None, None),
        P(("seq", "exp"), None, None),
    )
    out_specs = P("exp", "seq", None)
    return jax.shard_map(shards, mesh=mesh, in_specs=in_specs, out_specs=out_specs, check_vma=False)
```

profile of v0, /device:TPU:8, one launch (start us, length us, event | category | flops | bytes accessed | tf_op | source)
XLA Modules:
  0.0 670.7 jit_solution(1113696121236296590)
XLA Ops:
  13.8 4.5 gather_fusion
  18.4 47.6 %all-gather.4.cloned.1.call-done = bf16[1024,2048]{1,0:T(8,128)(2,1)} async-done(((bf16[128,2048]{1,0:T(8,128)(2,1)}), bf16[1024,2048]{1,0:T(8,128)(2,1)}) %all-gather.4.cloned.1.call-update) | async-done | bytes 4194320 | tf_op jit(solution)/shard_map/all_gather | solution.py:51
  71.8 33.6 %all-gather.6.cloned.1.call-done = bf16[1024,512]{1,0:T(8,128)(2,1)} async-done(((bf16[128,512]{1,0:T(8,128)(2,1)}), bf16[1024,512]{1,0:T(8,128)(2,1)}) %all-gather.6.cloned.1.call-update) | async-done | bytes 1048592 | tf_op jit(solution)/shard_map/all_gather | solution.py:60
  116.1 4.1 fusion.20
  120.2 4.1 fusion.19
  124.3 5.7 fusion.34
  131.9 4.9 reduce-window.6
  139.4 82.8 %reduce-scatter.3.cloned.1.call-done = f32[128,2048]{1,0:T(8,128)} async-done(((f32[1024,2048]{1,0:T(8,128)}), f32[128,2048]{1,0:T(8,128)}) %reduce-scatter.3.cloned.1.call-update) | async-done | bytes 1048592 | tf_op jit(solution)/shard_map/reduce_scatter | solution.py:81
  227.3 6.3 reshape.203
  233.6 10.4 %scatter_custom_fusion = bf16[1024,2048]{1,0:T(8,128)(2,1)} fusion(s32[768]{0:T(1024)S(1)} %fusion.46, bf16[768,2048]{1,0:T(8,128)(2,1)} %reshape.203, bf16[]{:T(256)} %constant.57.clone.1), kind=kCustom, calls=%fused_computation.25 | custom fusion | bytes 4194816 | tf_op jit(solution)/shard_map/scatter | solution.py:115
  244.1 6.8 %broadcast_in_dim.50 = bf16[64,2,16,2048]{3,2,1,0:T(8,128)(2,1)} broadcast(bf16[64,16,2048]{2,1,0:T(8,128)(2,1)} %bitcast.100), dimensions={0,2,3} | broadcast | bytes 12582912 | tf_op jit(solution)/shard_map/broadcast_in_dim | solution.py:117
  250.8 7.3 %all-to-all-start = ((bf16[128,16,2048]{2,1,0:T(8,128)(2,1)}), bf16[128,16,2048]{2,1,0:T(8,128)(2,1)}, u32[]{:S(2)}, u32[]{:S(2)}) async-start(bf16[128,16,2048]{2,1,0:T(8,128)(2,1)} %bitcast.99), calls=%async_computation.2 | async-start | bytes 16777216 | tf_op jit(solution)/shard_map/all_to_all | solution.py:118
  258.7 130.7 %all-to-all-done = bf16[128,16,2048]{2,1,0:T(8,128)(2,1)} async-done(((bf16[128,16,2048]{2,1,0:T(8,128)(2,1)}), bf16[128,16,2048]{2,1,0:T(8,128)(2,1)}, u32[]{:S(2)}, u32[]{:S(2)}) %all-to-all-start) | async-done | bytes 8388640 | tf_op jit(solution)/shard_map/all_to_all | solution.py:118
  389.4 11.2 %fusion.7 = f32[2048,704]{0,1:T(8,128)} fusion(bf16[2048,2048]{1,0:T(8,128)(2,1)} %bitcast.16, bf16[1,2048,704]{1,2,0:T(8,128)(2,1)} %param.33), kind=kOutput, calls=%fused_computation.22 | convolution fusion | flops 5905580032 | bytes 17039360 | tf_op jit(solution)/shard_map/dot_general | solution.py:21
  400.6 19.1 %convolution_convert_fusion = bf16[2048,2048]{1,0:T(8,128)(2,1)} fusion(f32[2048,704]{0,1:T(8,128)} %fusion.7, bf16[2048,2048]{1,0:T(8,128)(2,1)} %bitcast.16, bf16[1,704,2048]{2,1,0:T(8,128)(2,1)S(1)} %copy-done, bf16[1,2048,704]{1,2,0:T(8,128)(2,1)} %param.34), kind=kOutput, calls=%fused_computation.8 | convolution fusion | flops 11824005120 | bytes 28311552 | tf_op jit(solution)/shard_map/dot_general | solution.py:121
  419.7 43.2 %all-to-all-start.1 = ((bf16[128,16,2048]{2,1,0:T(8,128)(2,1)}), bf16[128,16,2048]{2,1,0:T(8,128)(2,1)}, u32[]{:S(2)}, u32[]{:S(2)}) async-start(bf16[128,16,2048]{2,1,0:T(8,128)(2,1)} %bitcast.101), calls=%async_computation.3 | async-start | bytes 16777216 | tf_op jit(solution)/shard_map/all_to_all | solution.py:125
  463.2 5.2 fusion.53
  468.4 9.0 %convolution_convert_fusion.1 = bf16[1024,2048]{1,0:T(8,128)(2,1)} fusion(bf16[352,2048]{1,0:T(8,128)(2,1)S(1)} %copy-done.16, bf16[1024,2048]{1,0:T(8,128)(2,1)} %all-gather.8.cloned.1.call-done, bf16[2048,352]{0,1:T(8,128)(2,1)} %param.31, f32[1024,352]{0,1:T(8,128)} %fusion.53), kind=kOutput, calls=%fused_computation.17 | convolution fusion | flops 2957049856 | bytes 12713984 | tf_op jit(solution)/shard_map/dot_general | solution.py:94
  478.2 140.0 %all-to-all-done.1 = bf16[128,16,2048]{2,1,0:T(8,128)(2,1)} async-done(((bf16[128,16,2048]{2,1,0:T(8,128)(2,1)}), bf16[128,16,2048]{2,1,0:T(8,128)(2,1)}, u32[]{:S(2)}, u32[]{:S(2)}) %all-to-all-start.1) | async-done | bytes 8388640 | tf_op jit(solution)/shard_map/all_to_all | solution.py:125
  618.2 11.3 %convert.3 = f32[64,2,16,2048]{3,2,1,0:T(8,128)} convert(bf16[64,2,16,2048]{3,2,1,0:T(8,128)(2,1)} %bitcast.22) | non-fusion elementwise | flops 4194304 | bytes 25165824 | tf_op jit(solution)/shard_map/convert_element_type | solution.py:128
  629.5 8.8 %fusion.1 = bf16[64,1,16,2048]{3,2,0,1:T(8,128)(2,1)} fusion(f32[64,2,16,2048]{3,2,1,0:T(8,128)} %convert.3), kind=kLoop, calls=%fused_computation.5 | loop fusion | flops 4194304 | bytes 20971520 | tf_op jit(solution)/shard_map/convert_element_type | solution.py:129
  638.3 9.8 %gather_fusion.1 = bf16[768,2048]{1,0:T(8,128)(2,1)} fusion(bf16[1024,2048]{1,0:T(8,128)(2,1)} %bitcast.98, s32[1024]{0:T(1024)S(1)} %pad_clamp_fusion), kind=kCustom, calls=%fused_computation.1 | custom fusion | bytes 6294528 | tf_op jit(solution)/shard_map/jit(_take)/gather | solution.py:130
  648.1 6.4 gather.15
  654.6 7.0 %multiply_reduce_fusion = f32[128,2048]{1,0:T(8,128)} fusion(f32[128,6]{1,0:T(8,128)S(1)} %bitcast.105, bf16[128,6,2048]{2,1,0:T(8,128)(2,1)} %gather.15, pred[128,6]{1,0:T(8,128)(4,1)S(1)} %copy.41), kind=kLoop, calls=%fused_computation.7 | loop fusion | flops 6029312 | bytes 4198144 | tf_op jit(solution)/shard_map/reduce_sum | solution.py:132
  (86 shorter events, 37.1 us)
Async XLA Ops:
  6.5 394.0 %copy-start = (bf16[1,704,2048]{2,1,0:T(8,128)(2,1)S(1)}, bf16[1,704,2048]{2,1,0:T(8,128)(2,1)}, u32[]{:S(2)}) copy-start(bf16[1,704,2048]{2,1,0:T(8,128)(2,1)} %param.35) | copy-start | bytes 8650756
  6.5 7.2 %copy-start.11 = (s32[1,1024]{1,0:T(1,128)S(1)}, s32[1,1024]{1,0:T(1,128)}, u32[]{:S(2)}) copy-start(s32[1,1024]{1,0:T(1,128)} %param.19) | copy-start | bytes 12292
  6.5 7.2 %copy-start.2 = (s32[1,1024]{1,0:T(1,128)S(1)}, s32[1,1024]{1,0:T(1,128)}, u32[]{:S(2)}) copy-start(s32[1,1024]{1,0:T(1,128)} %param.20) | copy-start | bytes 12292
  6.5 59.4 %all-gather.4.cloned.1.call-start = ((), (), s32[]{:S(2)}) async-start(), calls=%async_computation.4 | async-start | bytes 4718592 | tf_op jit(solution)/shard_map/all_gather | solution.py:51
  10.7 94.7 %all-gather.6.cloned.1.call-start = ((), (), s32[]{:S(2)}) async-start(), calls=%async_computation.5 | async-start | bytes 1179648 | tf_op jit(solution)/shard_map/all_gather | solution.py:60
  13.7 208.5 %reduce-scatter.3.cloned.1.call-start = ((), (), s32[]{:S(2)}) async-start(), calls=%async_computation.6 | async-start | bytes 9437184 | tf_op jit(solution)/shard_map/reduce_scatter | solution.py:81
  18.3 51.4 %copy-start.10 = (bf16[512,256]{1,0:T(8,128)(2,1)S(1)}, bf16[512,256]{1,0:T(8,128)(2,1)}, u32[]{:S(2)}) copy-start(bf16[512,256]{1,0:T(8,128)(2,1)} %param.27) | copy-start | bytes 786436
  108.6 5.0 copy-start.7
  108.6 3.1 copy-start.9
  108.6 3.4 copy-start.17
  113.6 1.9 copy-start.8
  130.1 0.7 copy-start.12
  130.1 1.1 copy-start.13
  130.1 92.1 %copy-start.3 = (bf16[1,128,2048]{2,1,0:T(8,128)(2,1)S(1)}, bf16[1,128,2048]{2,1,0:T(8,128)(2,1)}, u32[]{:S(2)}) copy-start(bf16[1,128,2048]{2,1,0:T(8,128)(2,1)} %param.18) | copy-start | bytes 1572868
  223.7 0.8 copy-start.4
  224.7 8.9 %copy-start.6 = (bf16[128,2048]{1,0:T(8,128)(2,1)}, bf16[128,2048]{1,0:T(8,128)(2,1)S(1)}, u32[]{:S(2)}) copy-start(bf16[128,2048]{1,0:T(8,128)(2,1)S(1)} %fusion.23) | copy-start | bytes 1572868
  250.8 138.5 %all-to-all-start = ((bf16[128,16,2048]{2,1,0:T(8,128)(2,1)}), bf16[128,16,2048]{2,1,0:T(8,128)(2,1)}, u32[]{:S(2)}, u32[]{:S(2)}) async-start(bf16[128,16,2048]{2,1,0:T(8,128)(2,1)} %bitcast.99), calls=%async_computation.2 | async-start | bytes 16777216 | tf_op jit(solution)/shard_map/all_to_all | solution.py:118
  258.1 205.1 %all-gather.8.cloned.1.call-start = ((), (), s32[]{:S(2)}) async-start(), calls=%async_computation.7 | async-start | bytes 4718592 | tf_op jit(solution)/shard_map/all_gather | solution.py:90
  419.7 43.5 %copy-start.15 = (bf16[2048,352]{0,1:T(8,128)(2,1)S(1)}, bf16[2048,352]{0,1:T(8,128)(2,1)}, u32[]{:S(2)}) copy-start(bf16[2048,352]{0,1:T(8,128)(2,1)} %param.30) | copy-start | bytes 4325380
  419.7 198.6 %all-to-all-start.1 = ((bf16[128,16,2048]{2,1,0:T(8,128)(2,1)}), bf16[128,16,2048]{2,1,0:T(8,128)(2,1)}, u32[]{:S(2)}, u32[]{:S(2)}) async-start(bf16[128,16,2048]{2,1,0:T(8,128)(2,1)} %bitcast.101), calls=%async_computation.3 | async-start | bytes 16777216 | tf_op jit(solution)/shard_map/all_to_all | solution.py:125
  462.9 5.5 copy-start.16
  462.9 198.6 %reduce-scatter.5.cloned.1.call-start = ((), (), s32[]{:S(2)}) async-start(), calls=%async_computation.8 | async-start | bytes 4718592 | tf_op jit(solution)/shard_map/reduce_scatter | solution.py:93
  648.1 15.7 %copy-start.1 = (bf16[1,704,2048]{2,1,0:T(8,128)(2,1)S(1)}, bf16[1,704,2048]{2,1,0:T(8,128)(2,1)}, u32[]{:S(2)}) copy-start(bf16[1,704,2048]{2,1,0:T(8,128)(2,1)} %param.35) | copy-start | bytes 8650756
  654.6 7.0 %copy-start.5 = (bf16[128,2048]{1,0:T(8,128)(2,1)S(1)}, bf16[128,2048]{1,0:T(8,128)(2,1)}, u32[]{:S(2)}) copy-start(bf16[128,2048]{1,0:T(8,128)(2,1)} %copy-done.4) | copy-start | bytes 1572868
  (1 other events, 0.7 us)
Sparse Core Ops, SparseCore 0:
  10.9 55.0 all-gather.3
  67.6 37.7 all-gather.5
  130.2 91.9 reduce-scatter.2
  260.3 144.3 all-gather.7
  477.5 143.9 reduce-scatter.4
where the time goes:
time: 680 us; the launch traced here: 671 us
  waiting for transfers between devices  435 us (64%)
  matrix products  71.9 us (11%)
  local copies, waits for them, and re-layouts  55.6 us (8%)
  starting transfers between devices  50.9 us (7%)
  other arithmetic  43.3 us (6%)
  between operations  13.7 us (2%)
    all_to_all x1, waiting for transfers between devices, shards(): lax.all_to_all(partial_value, ('seq', 'exp'), split_axis=0, concat_axis=0...  140 us
    all_to_all x1, waiting for transfers between devices, shards(): lax.all_to_all(doubled, ('seq', 'exp'), split_axis=0, concat_axis=0, tile...  131 us
    reduce_scatter x1, waiting for transfers between devices, shards(): lax.psum_scatter(jnp.dot(row_block, w_output, preferred_element_type=jnp....  82.8 us
    all_gather x1, waiting for transfers between devices, shards(): piece_rows = lax.all_gather(normed, 'seq', axis=0, tiled=True)  47.6 us
    all_to_all x1, starting transfers between devices, shards(): lax.all_to_all(partial_value, ('seq', 'exp'), split_axis=0, concat_axis=0...  43.2 us
    all_gather x1, waiting for transfers between devices, shards(): latent_all = lax.all_gather(latent_own, 'seq', axis=0, tiled=True)  33.6 us
    dot_general x1, matrix products, shards(): jnp.dot(activated, w_routed_down[0], preferred_element_type=jnp.float32)  19.1 us
    dot_general x2, matrix products, swiglu_rows(): jnp.dot(rows_in, gate_weight, preferred_element_type=jnp.float32)  16.4 us
  transfers between devices with their start and end apart: 7, of which 5 were waited for; matrix products, arithmetic and copies ran while one was open for 16% of the time, Pallas kernels for 0%

commit v1 on v0

--- a/solution.py
+++ b/solution.py
@@ -57,7 +57,9 @@
     ).astype(jnp.bfloat16)
     query_all = queries_query_latent.reshape(piece_rows.shape[0], heads_here * LAT)
     latent_own = jnp.dot(normed, w_latent, preferred_element_type=jnp.float32).astype(jnp.bfloat16)
-    latent_all = lax.all_gather(latent_own, "seq", axis=0, tiled=True)
+    latent_all = jnp.concatenate(
+        lax.all_to_all(jnp.stack([latent_own] * lax.axis_size("seq")), "seq", 0, 0), axis=0
+    )
     positions = position_of_row[0]
     requests = jnp.take(request_of_position[0], positions)
     allowed = (requests[:, None] == requests[None, :]) & (positions[None, :] <= positions[:, None])

time: 680 us -> 659 us (0.969)
  waiting for transfers between devices: 435 us -> 409 us
    all_gather x1 -> x0, waiting for transfers between devices: 33.6 us -> none  [shards(): latent_all = lax.all_gather(latent_own, 'seq', axis=0, tiled=True)]
  transfers between devices with their start and end apart: 7 -> 7, of which waited for: 5 -> 4; matrix products, arithmetic and copies ran while one was open for 16% -> 17% of each run, Pallas kernels for 0% -> 0%
where the time goes in v1:
time: 659 us; the launch traced here: 649 us
  waiting for transfers between devices  409 us (62%)
  matrix products  75.3 us (11%)
  starting transfers between devices  54 us (8%)
  local copies, waits for them, and re-layouts  52 us (8%)
  other arithmetic  45.5 us (7%)
  between operations  13.7 us (2%)
    all_to_all x1, waiting for transfers between devices, shards(): lax.all_to_all(partial_value, ('seq', 'exp'), split_axis=0, concat_axis=0...  140 us
    all_to_all x1, waiting for transfers between devices, shards(): lax.all_to_all(doubled, ('seq', 'exp'), split_axis=0, concat_axis=0, tile...  134 us
    reduce_scatter x1, waiting for transfers between devices, shards(): lax.psum_scatter(jnp.dot(row_block, w_output, preferred_element_type=jnp....  82.9 us
    all_gather x1, waiting for transfers between devices, shards(): piece_rows = lax.all_gather(normed, 'seq', axis=0, tiled=True)  51 us
    all_to_all x1, starting transfers between devices, shards(): lax.all_to_all(partial_value, ('seq', 'exp'), split_axis=0, concat_axis=0...  40.1 us
    dot_general x1, matrix products, shards(): jnp.dot(activated, w_routed_down[0], preferred_element_type=jnp.float32)  19.1 us
    dot_general x2, matrix products, swiglu_rows(): jnp.dot(rows_in, gate_weight, preferred_element_type=jnp.float32)  16.4 us
    gather x2, local copies, waits for them, and re-layouts, shards(): jnp.take(expert_out.reshape(experts * capacity, width), place, axis=0)  16.3 us
  transfers between devices with their start and end apart: 7, of which 4 were waited for; matrix products, arithmetic and copies ran while one was open for 17% of the time, Pallas kernels for 0%

profile of v1, /device:TPU:8, one launch (start us, length us, event | category | flops | bytes accessed | tf_op | source)
XLA Modules:
  0.0 649.1 jit_solution(2189730739884686604)
XLA Ops:
  14.0 6.2 all-to-all-start
  20.4 4.5 gather_fusion
  24.9 51.0 %all-gather.3.cloned.1.call-done = bf16[1024,2048]{1,0:T(8,128)(2,1)} async-done(((bf16[128,2048]{1,0:T(8,128)(2,1)}), bf16[1024,2048]{1,0:T(8,128)(2,1)}) %all-gather.3.cloned.1.call-update) | async-done | bytes 4194320 | tf_op jit(solution)/shard_map/all_gather | solution.py:51
  85.2 5.5 fusion.51
  91.3 4.1 fusion.20
  102.3 5.7 fusion.34
  109.9 4.9 reduce-window.6
  117.4 82.9 %reduce-scatter.3.cloned.1.call-done = f32[128,2048]{1,0:T(8,128)} async-done(((f32[1024,2048]{1,0:T(8,128)}), f32[128,2048]{1,0:T(8,128)}) %reduce-scatter.3.cloned.1.call-update) | async-done | bytes 1048592 | tf_op jit(solution)/shard_map/reduce_scatter | solution.py:83
  205.4 6.3 reshape.209
  211.7 10.4 %scatter_custom_fusion = bf16[1024,2048]{1,0:T(8,128)(2,1)} fusion(s32[768]{0:T(1024)S(1)} %fusion.46, bf16[768,2048]{1,0:T(8,128)(2,1)} %reshape.209, bf16[]{:T(256)} %constant.57.clone.1), kind=kCustom, calls=%fused_computation.25 | custom fusion | bytes 4194816 | tf_op jit(solution)/shard_map/scatter | solution.py:117
  222.1 6.8 %broadcast_in_dim.50 = bf16[64,2,16,2048]{3,2,1,0:T(8,128)(2,1)} broadcast(bf16[64,16,2048]{2,1,0:T(8,128)(2,1)} %bitcast.101), dimensions={0,2,3} | broadcast | bytes 12582912 | tf_op jit(solution)/shard_map/broadcast_in_dim | solution.py:119
  228.9 7.3 %all-to-all-start.1 = ((bf16[128,16,2048]{2,1,0:T(8,128)(2,1)}), bf16[128,16,2048]{2,1,0:T(8,128)(2,1)}, u32[]{:S(2)}, u32[]{:S(2)}) async-start(bf16[128,16,2048]{2,1,0:T(8,128)(2,1)} %bitcast.100), calls=%async_computation.3 | async-start | bytes 16777216 | tf_op jit(solution)/shard_map/all_to_all | solution.py:120
  236.9 134.2 %all-to-all-done.1 = bf16[128,16,2048]{2,1,0:T(8,128)(2,1)} async-done(((bf16[128,16,2048]{2,1,0:T(8,128)(2,1)}), bf16[128,16,2048]{2,1,0:T(8,128)(2,1)}, u32[]{:S(2)}, u32[]{:S(2)}) %all-to-all-start.1) | async-done | bytes 8388640 | tf_op jit(solution)/shard_map/all_to_all | solution.py:120
  371.1 11.2 %fusion.7 = f32[2048,704]{0,1:T(8,128)} fusion(bf16[2048,2048]{1,0:T(8,128)(2,1)} %bitcast.17, bf16[1,2048,704]{1,2,0:T(8,128)(2,1)} %param.33), kind=kOutput, calls=%fused_computation.22 | convolution fusion | flops 5905580032 | bytes 17039360 | tf_op jit(solution)/shard_map/dot_general | solution.py:21
  382.3 19.1 %convolution_convert_fusion = bf16[2048,2048]{1,0:T(8,128)(2,1)} fusion(f32[2048,704]{0,1:T(8,128)} %fusion.7, bf16[2048,2048]{1,0:T(8,128)(2,1)} %bitcast.17, bf16[1,704,2048]{2,1,0:T(8,128)(2,1)S(1)} %copy-done, bf16[1,2048,704]{1,2,0:T(8,128)(2,1)} %param.34), kind=kOutput, calls=%fused_computation.8 | convolution fusion | flops 11824005120 | bytes 28311552 | tf_op jit(solution)/shard_map/dot_general | solution.py:123
  401.4 40.1 %all-to-all-start.2 = ((bf16[128,16,2048]{2,1,0:T(8,128)(2,1)}), bf16[128,16,2048]{2,1,0:T(8,128)(2,1)}, u32[]{:S(2)}, u32[]{:S(2)}) async-start(bf16[128,16,2048]{2,1,0:T(8,128)(2,1)} %bitcast.102), calls=%async_computation.4 | async-start | bytes 16777216 | tf_op jit(solution)/shard_map/all_to_all | solution.py:127
  441.8 5.2 fusion.53
  447.0 9.0 %convolution_convert_fusion.1 = bf16[1024,2048]{1,0:T(8,128)(2,1)} fusion(bf16[352,2048]{1,0:T(8,128)(2,1)S(1)} %copy-done.15, bf16[1024,2048]{1,0:T(8,128)(2,1)} %all-gather.5.cloned.1.call-done, bf16[2048,352]{0,1:T(8,128)(2,1)} %param.31, f32[1024,352]{0,1:T(8,128)} %fusion.53), kind=kOutput, calls=%fused_computation.17 | convolution fusion | flops 2957049856 | bytes 12713984 | tf_op jit(solution)/shard_map/dot_general | solution.py:96
  456.8 139.8 %all-to-all-done.2 = bf16[128,16,2048]{2,1,0:T(8,128)(2,1)} async-done(((bf16[128,16,2048]{2,1,0:T(8,128)(2,1)}), bf16[128,16,2048]{2,1,0:T(8,128)(2,1)}, u32[]{:S(2)}, u32[]{:S(2)}) %all-to-all-start.2) | async-done | bytes 8388640 | tf_op jit(solution)/shard_map/all_to_all | solution.py:127
  596.7 11.3 %convert.3 = f32[64,2,16,2048]{3,2,1,0:T(8,128)} convert(bf16[64,2,16,2048]{3,2,1,0:T(8,128)(2,1)} %bitcast.23) | non-fusion elementwise | flops 4194304 | bytes 25165824 | tf_op jit(solution)/shard_map/convert_element_type | solution.py:130
  608.0 8.8 %fusion.1 = bf16[64,1,16,2048]{3,2,0,1:T(8,128)(2,1)} fusion(f32[64,2,16,2048]{3,2,1,0:T(8,128)} %convert.3), kind=kLoop, calls=%fused_computation.5 | loop fusion | flops 4194304 | bytes 20971520 | tf_op jit(solution)/shard_map/convert_element_type | solution.py:131
  616.8 9.8 %gather_fusion.1 = bf16[768,2048]{1,0:T(8,128)(2,1)} fusion(bf16[1024,2048]{1,0:T(8,128)(2,1)} %bitcast.99, s32[1024]{0:T(1024)S(1)} %pad_clamp_fusion), kind=kCustom, calls=%fused_computation.1 | custom fusion | bytes 6294528 | tf_op jit(solution)/shard_map/jit(_take)/gather | solution.py:132
  626.6 6.4 gather.15
  633.0 7.0 %multiply_reduce_fusion = f32[128,2048]{1,0:T(8,128)} fusion(f32[128,6]{1,0:T(8,128)S(1)} %bitcast.106, bf16[128,6,2048]{2,1,0:T(8,128)(2,1)} %gather.15, pred[128,6]{1,0:T(8,128)(4,1)S(1)} %copy.41), kind=kLoop, calls=%fused_computation.7 | loop fusion | flops 6029312 | bytes 4198144 | tf_op jit(solution)/shard_map/reduce_sum | solution.py:134
  (82 shorter events, 37.8 us)
Async XLA Ops:
  6.5 375.8 %copy-start = (bf16[1,704,2048]{2,1,0:T(8,128)(2,1)S(1)}, bf16[1,704,2048]{2,1,0:T(8,128)(2,1)}, u32[]{:S(2)}) copy-start(bf16[1,704,2048]{2,1,0:T(8,128)(2,1)} %param.35) | copy-start | bytes 8650756
  6.5 13.8 %copy-start.10 = (s32[1,1024]{1,0:T(1,128)S(1)}, s32[1,1024]{1,0:T(1,128)}, u32[]{:S(2)}) copy-start(s32[1,1024]{1,0:T(1,128)} %param.19) | copy-start | bytes 12292
  6.5 13.8 %copy-start.2 = (s32[1,1024]{1,0:T(1,128)S(1)}, s32[1,1024]{1,0:T(1,128)}, u32[]{:S(2)}) copy-start(s32[1,1024]{1,0:T(1,128)} %param.20) | copy-start | bytes 12292
  6.5 69.5 %all-gather.3.cloned.1.call-start = ((), (), s32[]{:S(2)}) async-start(), calls=%async_computation.5 | async-start | bytes 4718592 | tf_op jit(solution)/shard_map/all_gather | solution.py:51
  14.0 67.8 %all-to-all-start = ((bf16[8,128,512]{2,1,0:T(8,128)(2,1)}), bf16[8,128,512]{2,1,0:T(8,128)(2,1)}, u32[]{:S(2)}, u32[]{:S(2)}) async-start(bf16[8,128,512]{2,1,0:T(8,128)(2,1)} %stack.2), calls=%async_computation | async-start | bytes 2097152 | tf_op jit(solution)/shard_map/all_to_all | solution.py:61
  20.3 180.0 %reduce-scatter.3.cloned.1.call-start = ((), (), s32[]{:S(2)}) async-start(), calls=%async_computation.6 | async-start | bytes 9437184 | tf_op jit(solution)/shard_map/reduce_scatter | solution.py:83
  24.9 54.8 %copy-start.9 = (bf16[512,256]{1,0:T(8,128)(2,1)S(1)}, bf16[512,256]{1,0:T(8,128)(2,1)}, u32[]{:S(2)}) copy-start(bf16[512,256]{1,0:T(8,128)(2,1)} %param.27) | copy-start | bytes 786436
  81.8 3.3 copy-start.8
  85.2 5.5 copy-start.7
  108.1 0.7 copy-start.11
  108.1 1.1 copy-start.12
  108.1 92.2 %copy-start.3 = (bf16[1,128,2048]{2,1,0:T(8,128)(2,1)S(1)}, bf16[1,128,2048]{2,1,0:T(8,128)(2,1)}, u32[]{:S(2)}) copy-start(bf16[1,128,2048]{2,1,0:T(8,128)(2,1)} %param.18) | copy-start | bytes 1572868
  201.8 0.8 copy-start.4
  202.8 8.9 %copy-start.6 = (bf16[128,2048]{1,0:T(8,128)(2,1)}, bf16[128,2048]{1,0:T(8,128)(2,1)S(1)}, u32[]{:S(2)}) copy-start(bf16[128,2048]{1,0:T(8,128)(2,1)S(1)} %fusion.23) | copy-start | bytes 1572868
  228.9 142.2 %all-to-all-start.1 = ((bf16[128,16,2048]{2,1,0:T(8,128)(2,1)}), bf16[128,16,2048]{2,1,0:T(8,128)(2,1)}, u32[]{:S(2)}, u32[]{:S(2)}) async-start(bf16[128,16,2048]{2,1,0:T(8,128)(2,1)} %bitcast.100), calls=%async_computation.3 | async-start | bytes 16777216 | tf_op jit(solution)/shard_map/all_to_all | solution.py:120
  236.2 205.6 %all-gather.5.cloned.1.call-start = ((), (), s32[]{:S(2)}) async-start(), calls=%async_computation.7 | async-start | bytes 4718592 | tf_op jit(solution)/shard_map/all_gather | solution.py:92
  401.4 40.4 %copy-start.14 = (bf16[2048,352]{0,1:T(8,128)(2,1)S(1)}, bf16[2048,352]{0,1:T(8,128)(2,1)}, u32[]{:S(2)}) copy-start(bf16[2048,352]{0,1:T(8,128)(2,1)} %param.30) | copy-start | bytes 4325380
  401.4 195.3 %all-to-all-start.2 = ((bf16[128,16,2048]{2,1,0:T(8,128)(2,1)}), bf16[128,16,2048]{2,1,0:T(8,128)(2,1)}, u32[]{:S(2)}, u32[]{:S(2)}) async-start(bf16[128,16,2048]{2,1,0:T(8,128)(2,1)} %bitcast.102), calls=%async_computation.4 | async-start | bytes 16777216 | tf_op jit(solution)/shard_map/all_to_all | solution.py:127
  441.5 5.5 copy-start.15
  441.5 198.4 %reduce-scatter.5.cloned.1.call-start = ((), (), s32[]{:S(2)}) async-start(), calls=%async_computation.8 | async-start | bytes 4718592 | tf_op jit(solution)/shard_map/reduce_scatter | solution.py:95
  456.0 0.7 copy-start.13
  626.6 15.7 %copy-start.1 = (bf16[1,704,2048]{2,1,0:T(8,128)(2,1)S(1)}, bf16[1,704,2048]{2,1,0:T(8,128)(2,1)}, u32[]{:S(2)}) copy-start(bf16[1,704,2048]{2,1,0:T(8,128)(2,1)} %param.35) | copy-start | bytes 8650756
  633.0 7.0 %copy-start.5 = (bf16[128,2048]{1,0:T(8,128)(2,1)S(1)}, bf16[128,2048]{1,0:T(8,128)(2,1)}, u32[]{:S(2)}) copy-start(bf16[128,2048]{1,0:T(8,128)(2,1)} %copy-done.4) | copy-start | bytes 1572868
Sparse Core Ops, SparseCore 0:
  10.9 65.0 all-gather.2
  108.2 92.0 reduce-scatter.2
  238.7 146.0 all-gather.4
  456.2 143.7 reduce-scatter.4
